TPU v7x, 32 devices: a whole 2x2x4 slice. The times are simulated.
32 devices in a mesh: param: 16 (over z, y, x), trace: 2 (over core).
Axes of the slice: x: 2, y: 2, z: 4, core: 2. Of those that a mesh axis runs over, the one named last changes fastest.
Arguments:
- grads: bfloat16 [8, 16777216], P('trace', 'param'), may hold values from -6 to 6
- signs: int32 [16777216], P('param'), may hold values 0 or 1
- kept: int32 [512], replicated, may hold values from 0 to 131071, as said below
Outputs:
- features: float32 [8, 65536], P(None, ('param', 'trace'))
Inputs may be any that keep to these rules, and one draw needn't show every extreme that they name: `kept`: 512 distinct block numbers.
All inputs are finite; a program needn't handle non-finite values. No bound on the sum of `signs` on one device may be relied on, other than what follows from the above.
Results may differ from a plain program's by a relative error of at most 0.0003.
Values sent between devices are 32-bit elements; how exact they have to be, the bound alone decides.
A program may use at most 192 MiB of HBM per device.

v0:
```python
import jax
import jax.numpy as jnp
from jax import lax
from jax.sharding import PartitionSpec as P

D = 4096
BLOCK = 128


def parity_signs(row_values, col_values, bit_count):
    intersection = row_values[:, None] & col_values[None, :]
    parity = jnp.zeros(intersection.shape, jnp.int32)
    for bit_number in range(bit_count):
        parity = parity + (intersection >> bit_number & 1)
    return 1 - 2 * (parity % 2)


def per_device(grads, signs, kept):
    traces, local_size = grads.shape
    groups = lax.axis_size("param")
    own_index = lax.axis_index("param")
    left_size = 2 ** ((local_size.bit_length() - 1) // 2)
    right_size = local_size // left_size
    left_table = parity_signs(
        jnp.arange(left_size, dtype=jnp.int32),
        jnp.arange(left_size, dtype=jnp.int32),
        left_size.bit_length(),
    ).astype(jnp.bfloat16)
    right_table = parity_signs(
        jnp.arange(right_size, dtype=jnp.int32),
        jnp.arange(right_size, dtype=jnp.int32),
        right_size.bit_length(),
    ).astype(jnp.float32)
    signed = jnp.where(signs[None, :] == 1, grads, -grads).reshape(traces, left_size, right_size)
    half_done = jnp.einsum("ij,tjk->tik", left_table, signed, preferred_element_type=jnp.float32)
    local_done = jnp.einsum("tik,kl->til", half_done, right_table, precision=lax.Precision.HIGHEST)
    blocks_dev = local_size // BLOCK
    region = kept // blocks_dev
    within = kept % blocks_dev
    bit_count = groups.bit_length()
    per_width = local_size // groups
    columns = local_done.reshape(traces, groups, per_width)
    exchanged = lax.all_to_all(columns, "param", split_axis=1, concat_axis=1, tiled=True)
    device_table = parity_signs(
        jnp.arange(groups, dtype=jnp.int32), jnp.arange(groups, dtype=jnp.int32), bit_count
    ).astype(jnp.float32)
    mixed_full = jnp.einsum("ab,tbw->taw", device_table, exchanged, precision=lax.Precision.HIGHEST)
    per_block = per_width // BLOCK
    holder = within // per_block
    column = within % per_block
    spread = mixed_full.reshape(traces, groups * per_block, BLOCK)
    picked = jnp.take(spread, region * per_block + column, axis=1)
    picked = jnp.where((holder == own_index)[None, :, None], picked, 0.0)
    sent_terms = jnp.transpose(picked, (1, 0, 2))[:, None, :, :]
    received = lax.all_to_all(
        lax.all_to_all(sent_terms, "param", split_axis=0, concat_axis=1, tiled=True),
        "trace",
        split_axis=0,
        concat_axis=2,
        tiled=True,
    )
    owned = jnp.sum(received, axis=1)
    scaling = 1.0 / D
    blocks_here = owned.shape[0]
    return jnp.transpose(owned, (1, 0, 2)).reshape(owned.shape[1], blocks_here * BLOCK) * scaling


def solution(mesh):
    placed = (P("trace", "param"), P("param"), P())
    return jax.shard_map(
        per_device,
        mesh=mesh,
        in_specs=placed,
        out_specs=P(None, ("param", "trace")),
        check_vma=False,
    )
```

profile of v0, /device:TPU:1, one launch (start us, length us, event | category | flops | bytes accessed | tf_op | source)
XLA Modules:
  0.0 644.6 jit_solution(15995905488393154556)
XLA Ops:
  0.0 0.0 copy-start
  0.0 6.3 fusion.64
  6.3 2.7 broadcast_compare_fusion
  9.1 0.0 copy-done
  9.1 7.7 %negate_select_fusion = bf16[4,1048576]{1,0:T(4,128)(2,1)S(1)} fusion(bf16[4,1048576]{1,0:T(4,128)(2,1)S(1)} %copy-done, pred[1048576]{0:T(1024)(128)(4,1)S(1)} %broadcast_compare_fusion), kind=kLoop, calls=%fused_computation.5 | loop fusion | flops 8388608 | bytes 17825792 | tf_op jit(solution)/shard_map/jit(_where)/select_n | solution.py:34
  16.8 28.0 %fusion.3 = f32[4,1024,1024]{2,1,0:T(8,128)} fusion(bf16[1,4,1024,1024]{3,1,2,0:T(4,128)(2,1)S(1)} %bitcast.43), kind=kOutput, calls=%fused_computation.6 | convolution fusion | flops 8639217664 | bytes 25165824 | tf_op jit(solution)/shard_map/ij,tjk->tik/dot_general | solution.py:35
  44.8 59.7 %fusion = f32[4,1024,1024]{2,1,0:T(8,128)} fusion(f32[4,1024,1024]{2,1,0:T(8,128)} %fusion.3, f32[1024,1024,1]{1,0,2:T(8,128)S(1)} %fusion.64), kind=kOutput, calls=%fused_computation.2 | convolution fusion | flops 51539607552 | bytes 37748736 | tf_op jit(solution)/shard_map/tik,kl->til/dot_general | solution.py:36
  104.5 14.5 %reshape.25 = f32[4,16,65536]{2,1,0:T(8,128)} reshape(f32[4,1024,1024]{2,1,0:T(8,128)} %fusion) | data formatting | bytes 33554432 | tf_op jit(solution)/shard_map/reshape | solution.py:42
  119.1 20.9 %copy.21 = f32[4,16,65536]{2,0,1:T(4,128)} copy(f32[4,16,65536]{2,1,0:T(8,128)} %reshape.25) | data formatting | bytes 33554432 | tf_op jit(solution)/shard_map/reshape | solution.py:42
  140.0 0.0 copy-start.1
  140.0 7.6 %all-to-all-start = ((f32[4,16,65536]{2,0,1:T(4,128)}), f32[4,16,65536]{2,0,1:T(4,128)}, u32[]{:S(2)}, u32[]{:S(2)}) async-start(f32[4,16,65536]{2,0,1:T(4,128)} %copy.21), calls=%async_computation | async-start | bytes 33554432 | tf_op jit(solution)/shard_map/all_to_all | solution.py:43
  147.6 0.0 copy-done.1
  147.6 313.7 %all-to-all-done = f32[4,16,65536]{2,0,1:T(4,128)} async-done(((f32[4,16,65536]{2,0,1:T(4,128)}), f32[4,16,65536]{2,0,1:T(4,128)}, u32[]{:S(2)}, u32[]{:S(2)}) %all-to-all-start) | async-done | bytes 16777248 | tf_op jit(solution)/shard_map/all_to_all | solution.py:43
  461.3 32.1 %convolution_bitcast_fusion = f32[4,16,65536]{2,1,0:T(8,128)} fusion(f32[4,16,65536]{2,0,1:T(4,128)} %all-to-all-done), kind=kOutput, calls=%fused_computation.1 | convolution fusion | flops 805313792 | bytes 33554432 | tf_op jit(solution)/shard_map/ab,tbw->taw/dot_general | solution.py:47
  493.5 14.3 %reshape.26 = f32[4,8192,128]{2,1,0:T(8,128)} reshape(f32[4,16,65536]{2,1,0:T(8,128)} %convolution_bitcast_fusion) | data formatting | bytes 33554432 | tf_op jit(solution)/shard_map/reshape | solution.py:51
  507.8 20.9 %copy.23 = f32[4,8192,128]{2,0,1:T(4,128)} copy(f32[4,8192,128]{2,1,0:T(8,128)} %reshape.26) | data formatting | bytes 33554432 | tf_op jit(solution)/shard_map/reshape | solution.py:51
  528.7 7.3 %gather_fusion = f32[512,4,128]{2,1,0:T(4,128)S(1)} fusion(f32[4,8192,128]{2,0,1:T(4,128)} %copy.23, s32[1024]{0:T(1024)S(1)} %pad_clamp_fusion), kind=kCustom, calls=%fused_computation | custom fusion | bytes 2099200 | tf_op jit(solution)/shard_map/jit(_take)/gather | solution.py:52
  536.0 2.4 select_bitcast_fusion
  538.4 97.3 %all_to_all.32 = f32[512,1,4,128]{3,2,1,0:T(4,128)S(1)} all-to-all(f32[512,1,4,128]{3,2,1,0:T(4,128)S(1)} %select_bitcast_fusion), channel_id=1, replica_groups=mesh['param'=16,'trace'=2] {'param'}, dimensions={0} | all-to-all | bytes 2097152 | tf_op jit(solution)/shard_map/all_to_all | solution.py:56
  635.6 0.3 copy.43
  635.9 7.6 %all_to_all.33 = f32[32,16,4,128]{3,2,1,0:T(4,128)S(1)} all-to-all(f32[32,16,4,128]{3,2,1,0:T(4,128)S(1)} %bitcast.45), channel_id=1, replica_groups=mesh['param'=16,'trace'=2] {'trace'}, dimensions={0} | all-to-all | bytes 2097152 | tf_op jit(solution)/shard_map/all_to_all | solution.py:55
  643.5 0.2 reduce_sum.11
  643.7 0.7 copy.44
  (4 shorter events, 0.0 us)
Async XLA Ops:
  0.0 9.1 %copy-start = (bf16[4,1048576]{1,0:T(4,128)(2,1)S(1)}, bf16[4,1048576]{1,0:T(4,128)(2,1)}, u32[]{:S(2)}) copy-start(bf16[4,1048576]{1,0:T(4,128)(2,1)} %param.3) | copy-start | bytes 25165828
  140.0 7.6 %copy-start.1 = (s32[512]{0:T(512)S(1)}, s32[512]{0:T(512)}, u32[]{:S(2)}) copy-start(s32[512]{0:T(512)} %param.5) | copy-start | bytes 6148
  140.0 321.4 %all-to-all-start = ((f32[4,16,65536]{2,0,1:T(4,128)}), f32[4,16,65536]{2,0,1:T(4,128)}, u32[]{:S(2)}, u32[]{:S(2)}) async-start(f32[4,16,65536]{2,0,1:T(4,128)} %copy.21), calls=%async_computation | async-start | bytes 33554432 | tf_op jit(solution)/shard_map/all_to_all | solution.py:43
where the time goes:
time: 652 us; the launch traced here: 645 us
  waiting for transfers between devices  314 us (48%)
  matrix products  120 us (18%)
  blocking collectives  105 us (16%)
  local copies, waits for them, and re-layouts  78.9 us (12%)
  other arithmetic  19.3 us (3%)
  starting transfers between devices  7.6 us (1%)
    all_to_all x1, waiting for transfers between devices, per_device(): lax.all_to_all(columns, 'param', split_axis=1, concat_axis=1, tiled=True)  314 us
    all_to_all x1, blocking collectives, per_device(): lax.all_to_all(sent_terms, 'param', split_axis=0, concat_axis=1, tiled=True)  97.3 us
    dot_general x1, matrix products, per_device(): jnp.einsum('tik,kl->til', half_done, right_table, precision=lax.Precision...  59.7 us
    reshape x2, local copies, waits for them, and re-layouts, per_device(): columns = local_done.reshape(traces, groups, per_width)  35.4 us
    reshape x2, local copies, waits for them, and re-layouts, per_device(): spread = mixed_full.reshape(traces, groups * per_block, BLOCK)  35.2 us
    dot_general x1, matrix products, per_device(): jnp.einsum('ab,tbw->taw', device_table, exchanged, precision=lax.Precisio...  32.1 us
    dot_general x1, matrix products, per_device(): jnp.einsum('ij,tjk->tik', left_table, signed, preferred_element_type=jnp....  28 us
  transfers between devices with their start and end apart: 1, of which 1 were waited for; matrix products, arithmetic and copies ran while one was open for 0% of the time, Pallas kernels for 0%

commit v1 on v0

v1 whole, which is shorter than its diff:
```python
import functools

import jax
import jax.numpy as jnp
from jax import lax
from jax.experimental import pallas as pl
from jax.experimental.pallas import tpu as pltpu
from jax.sharding import PartitionSpec as P

D = 4096
BLOCK = 128
SUB = 8


def parity(value):
    for shift in (16, 8, 4, 2, 1):
        value = value ^ (value >> shift)
    return value & 1


def sign_of(value):
    return (1 - 2 * parity(value)).astype(jnp.float32).astype(jnp.bfloat16)


def partial_kernel(kept_ref, x_ref, s_ref, o_ref, low_ref, wide_ref):
    step = pl.program_id(0)
    rows = s_ref.shape[0]
    traces = x_ref.shape[0] // rows
    kept = kept_ref[...]

    @pl.when(step == 0)
    def _():
        lane = lax.broadcasted_iota(jnp.int32, kept.shape, 1)
        for k in range(SUB):
            low_ref[:, k * BLOCK:(k + 1) * BLOCK] = sign_of(kept & (lane + k * BLOCK))

    upper = lax.axis_index("param") * pl.num_programs(0) + step
    high = sign_of(kept & (upper * (SUB * BLOCK)))
    table = low_ref[...] * jnp.concatenate([high] * SUB, axis=1)
    wide_ref[...] = x_ref[...].astype(jnp.float32)
    sign = (2 * s_ref[...] - 1).astype(jnp.float32)
    signed = jnp.concatenate(
        [(wide_ref[pl.ds(t, rows, stride=traces), :] * sign).astype(jnp.bfloat16) for t in range(traces)],
        axis=1,
    )
    term = jnp.dot(table, signed, preferred_element_type=jnp.float32)

    @pl.when(step == 0)
    def _():
        o_ref[...] = term

    @pl.when(step > 0)
    def _():
        o_ref[...] += term


def partial_sums(grads, signs, kept):
    traces, local_size = grads.shape
    keep = kept.shape[0]
    blocks = local_size // BLOCK
    rows = SUB * BLOCK
    x = grads.reshape(traces, blocks, BLOCK).transpose(1, 0, 2).reshape(blocks * traces, BLOCK)
    s = signs.reshape(blocks, BLOCK)
    kept_wide = jnp.broadcast_to(kept[:, None], (keep, BLOCK))
    return pl.pallas_call(
        partial_kernel,
        out_shape=jax.ShapeDtypeStruct((keep, traces * BLOCK), jnp.float32),
        grid=(blocks // rows,),
        in_specs=[
            pl.BlockSpec((keep, BLOCK), lambda i: (0, 0)),
            pl.BlockSpec((rows * traces, BLOCK), lambda i: (i, 0)),
            pl.BlockSpec((rows, BLOCK), lambda i: (i, 0)),
        ],
        out_specs=pl.BlockSpec((keep, traces * BLOCK), lambda i: (0, 0)),
        scratch_shapes=[
            pltpu.VMEM((keep, rows), jnp.bfloat16),
            pltpu.VMEM((rows * traces, BLOCK), jnp.float32),
        ],
        compiler_params=pltpu.CompilerParams(
            dimension_semantics=("arbitrary",), vmem_limit_bytes=60 << 20
        ),
    )(kept_wide, x, s)


def lane_table():
    index = jnp.arange(BLOCK, dtype=jnp.int32)
    return (1 - 2 * parity(index[:, None] & index[None, :])).astype(jnp.float32) / D


def per_device(grads, signs, kept):
    sums = partial_sums(grads, signs, kept)
    mine = lax.psum_scatter(sums, "param", scatter_dimension=0, tiled=True)
    both = lax.all_to_all(mine, "trace", split_axis=0, concat_axis=1, tiled=True)
    here = both.shape[0]
    split = both.reshape(here, -1, BLOCK)
    done = jnp.einsum("ftl,lc->tfc", split, lane_table(), precision=lax.Precision.HIGHEST)
    return done.reshape(-1, here * BLOCK)


def solution(mesh):
    placed = (P("trace", "param"), P("param"), P())
    return jax.shard_map(
        per_device,
        mesh=mesh,
        in_specs=placed,
        out_specs=P(None, ("param", "trace")),
        check_vma=False,
    )
```

time: 652 us -> 115 us (0.18); the launches traced: 645 us -> 114 us
  waiting for transfers between devices: 314 us -> 68.6 us
  matrix products: 120 us -> 0.24 us
  blocking collectives: 105 us -> 16.5 us
  local copies, waits for them, and re-layouts: 78.9 us -> 2.28 us
  other arithmetic: 19.3 us -> 0 us
  Pallas kernels: 0 us -> 13.2 us
  between operations: 0.34 us -> 13.4 us
  starting transfers between devices: 7.6 us -> 0.01 us
    all_to_all x1 -> x0, waiting for transfers between devices: 314 us -> none  [per_device(): lax.all_to_all(columns, 'param', split_axis=1, concat_axis=1, tiled=True)]
    dot_general x3 -> x1, matrix products: 120 us -> 0.24 us  [per_device(): jnp.einsum('ftl,lc->tfc', split, lane_table(), precision=lax.Precision.HI...]
    all_to_all x2 -> x1, blocking collectives: 105 us -> 16.5 us  [per_device(): lax.all_to_all(mine, 'trace', split_axis=0, concat_axis=1, tiled=True)]
    reshape x4 -> x1, local copies, waits for them, and re-layouts: 70.6 us -> 0.05 us  [per_device(): split = both.reshape(here, -1, BLOCK)]
    reduce_scatter x0 -> x1, waiting for transfers between devices: none -> 68.6 us  [per_device(): mine = lax.psum_scatter(sums, 'param', scatter_dimension=0, tiled=True)]
    pallas_call x0 -> x1, Pallas kernels: none -> 13.2 us  [partial_sums(): pl.pallas_call(partial_kernel, out_shape=jax.ShapeDtypeStruct((keep, trac...]
    select_n x1 -> x0, other arithmetic: 7.68 us -> none  [per_device(): jnp.where(signs[None, :] == 1, grads, -grads)]
    all_to_all x1 -> x0, starting transfers between devices: 7.6 us -> none  [per_device(): lax.all_to_all(columns, 'param', split_axis=1, concat_axis=1, tiled=True)]
where the time goes in v1:
time: 115 us; the launch traced here: 114 us
  waiting for transfers between devices  68.6 us (60%)
  blocking collectives  16.5 us (14%)
  between operations  13.4 us (12%)
  Pallas kernels  13.2 us (11%)
  local copies, waits for them, and re-layouts  2.28 us (2%)
    reduce_scatter x1, waiting for transfers between devices, per_device(): mine = lax.psum_scatter(sums, 'param', scatter_dimension=0, tiled=True)  68.6 us
    all_to_all x1, blocking collectives, per_device(): lax.all_to_all(mine, 'trace', split_axis=0, concat_axis=1, tiled=True)  16.5 us
    pallas_call x1, Pallas kernels, partial_sums(): pl.pallas_call(partial_kernel, out_shape=jax.ShapeDtypeStruct((keep, trac...  13.2 us
  transfers between devices with their start and end apart: 1, of which 1 were waited for; matrix products, arithmetic and copies ran while one was open for 0% of the time, Pallas kernels for 0%

profile of v1, /device:TPU:1, one launch (start us, length us, event | category | flops | bytes accessed | tf_op | source)
XLA Modules:
  0.0 114.2 jit_solution(8252922085268464722)
XLA Ops:
  6.5 0.0 reduce-scatter.2.cloned.1.call-start
  6.5 1.5 %broadcast_in_dim.2.kept_ref = s32[512,128]{1,0:T(8,128)} broadcast(s32[512]{0:T(512)} %param.5), dimensions={0} | broadcast | bytes 264192 | tf_op jit(solution)/shard_map/broadcast_in_dim | solution.py:64
  8.1 13.2 %shard_map.37 = f32[512,512]{1,0:T(8,128)} custom-call(s32[512,128]{1,0:T(8,128)} %broadcast_in_dim.2.kept_ref, bf16[32768,128]{1,0:T(8,128)(2,1)} %bitcast.17, s32[8192,128]{1,0:T(8,128)} %bitcast.18), custom_call_target="tpu_custom_call" | custom-call | tf_op jit(solution)/shard_map/pallas_call | solution.py:65
  21.2 0.0 reduce-scatter.2.cloned.1.call-update
  21.3 68.6 %reduce-scatter.2.cloned.1.call-done = f32[32,512]{1,0:T(8,128)} async-done(((f32[512,512]{1,0:T(8,128)}), f32[32,512]{1,0:T(8,128)}) %reduce-scatter.2.cloned.1.call-update) | async-done | bytes 65552 | tf_op jit(solution)/shard_map/reduce_scatter | solution.py:92
  89.8 16.5 %all_to_all.16 = f32[2,16,512]{2,1,0:T(8,128)S(1)} all-to-all(f32[2,16,512]{2,1,0:T(8,128)} %bitcast.20), channel_id=1, replica_groups=mesh['param'=16,'trace'=2] {'trace'}, dimensions={0} | all-to-all | bytes 131072 | tf_op jit(solution)/shard_map/all_to_all | solution.py:93
  106.3 0.1 copy.9
  106.4 0.1 reshape.23
  106.4 0.2 convolution_bitcast_fusion
  106.7 0.7 copy.15
Async XLA Ops:
  6.5 83.3 %reduce-scatter.2.cloned.1.call-start = ((), (), s32[]{:S(2)}) async-start(), calls=%async_computation.2 | async-start | bytes 1114112 | tf_op jit(solution)/shard_map/reduce_scatter | solution.py:92
Sparse Core Ops, SparseCore 0:
  21.4 68.4 reduce-scatter.1

commit v2 on v1

--- a/solution.py
+++ b/solution.py
@@ -82,19 +82,158 @@
     )(kept_wide, x, s)
 
 
-def lane_table():
-    index = jnp.arange(BLOCK, dtype=jnp.int32)
-    return (1 - 2 * parity(index[:, None] & index[None, :])).astype(jnp.float32) / D
+def cut_of(groups):
+    bits = groups.bit_length() - 1
+    minor = bits // 3
+    return 2 ** (bits - 2 * minor), 2 ** minor, 2 ** minor
+
+
+def parts_of(width):
+    unit = width // 4
+    return (
+        (0, 2 * unit, (2, 1, 0)),
+        (2 * unit, unit, (1, 0, 2)),
+        (3 * unit, unit, (0, 2, 1)),
+    )
+
+
+def at_axis(ref, axis, index):
+    return ref.at[(slice(None),) * axis + (index,)]
+
+
+def combine_kernel(cut, parts, plan, sums_ref, o_ref, final_ref, other_ref, send_sem, recv_sem, *buffers):
+    own = lax.axis_index("param")
+    core = lax.axis_index("trace")
+    spans = (cut[1] * cut[2], cut[2], 1)
+    place = tuple((own // spans[d]) % cut[d] for d in range(3))
+
+    def peer(d, offset):
+        there = (place[d] + offset) % cut[d]
+        return there, own + (there - place[d]) * spans[d]
+
+    barrier = pltpu.get_barrier_semaphore()
+    count = 0
+    for d in range(3):
+        for offset in range(1, cut[d]):
+            pl.semaphore_signal(
+                barrier, inc=1, device_id={"param": peer(d, offset)[1]}, device_id_type=pl.DeviceIdType.MESH
+            )
+            count += 1
+    pl.semaphore_signal(barrier, inc=1, device_id={"trace": 1 - core}, device_id_type=pl.DeviceIdType.MESH)
+    pl.semaphore_wait(barrier, count + 1)
+
+    lanes = [pl.ds(low, width) for low, width, _ in parts]
+    held = [sums_ref.at[:, :, :, :, lanes[n]] for n in range(len(parts))]
+    flying = {}
+    sent = []
+
+    def launch(n, stage):
+        d, axis, slots, result, first = plan[n][stage]
+        copies = []
+        for offset in range(1, cut[d]):
+            there, device = peer(d, offset)
+            copy = pltpu.make_async_remote_copy(
+                src_ref=at_axis(held[n], axis, there),
+                dst_ref=buffers[slots].at[offset - 1],
+                send_sem=send_sem.at[first + offset - 1],
+                recv_sem=recv_sem.at[first + offset - 1],
+                device_id={"param": device},
+                device_id_type=pl.DeviceIdType.MESH,
+            )
+            copy.start()
+            copies.append(copy)
+        flying[n, stage] = copies
+        sent.extend(copies)
+
+    for n in range(len(parts)):
+        launch(n, 0)
+    for stage in range(3):
+        for n in range(len(parts)):
+            d, axis, slots, result, first = plan[n][stage]
+            total = at_axis(held[n], axis, place[d])[...]
+            for offset in range(1, cut[d]):
+                flying[n, stage][offset - 1].wait_recv()
+                total = total + buffers[slots][offset - 1]
+            if stage < 2:
+                buffers[result][...] = total
+                held[n] = buffers[result]
+                launch(n, stage + 1)
+            else:
+                final_ref[:, lanes[n]] = total
+
+    rows = final_ref.shape[0] // 2
+    here = other_ref.shape[0]
+    whole = here == 2 * rows
+    swap = pltpu.make_async_remote_copy(
+        src_ref=final_ref if whole else final_ref.at[pl.ds((1 - core) * rows, rows)],
+        dst_ref=other_ref,
+        send_sem=send_sem.at[send_sem.shape[0] - 1],
+        recv_sem=recv_sem.at[recv_sem.shape[0] - 1],
+        device_id={"trace": 1 - core},
+        device_id_type=pl.DeviceIdType.MESH,
+    )
+    swap.start()
+    mine = jnp.where(core == 0, final_ref[0:rows, :], final_ref[rows:2 * rows, :])
+    swap.wait_recv()
+    if whole:
+        theirs = jnp.where(core == 0, other_ref[0:rows, :], other_ref[rows:2 * rows, :])
+    else:
+        theirs = other_ref[...]
+    both = (jnp.where(core == 0, mine, theirs), jnp.where(core == 0, theirs, mine))
+    local = final_ref.shape[1] // BLOCK
+    for half in range(2):
+        for t in range(local):
+            o_ref[pl.ds(half * local + t, rows, stride=2 * local), :] = both[half][:, t * BLOCK:(t + 1) * BLOCK]
+    index = lax.broadcasted_iota(jnp.int32, (BLOCK, BLOCK), 0) & lax.broadcasted_iota(jnp.int32, (BLOCK, BLOCK), 1)
+    table = (1 - 2 * parity(index)).astype(jnp.float32) * (1.0 / D)
+    o_ref[...] = jnp.dot(
+        o_ref[...], table, precision=lax.Precision.HIGHEST, preferred_element_type=jnp.float32
+    )
+    for copy in sent:
+        copy.wait_send()
+    swap.wait_send()
+
+
+def combine(sums, groups):
+    keep, width = sums.shape
+    cut = cut_of(groups)
+    rows = keep // groups
+    parts = parts_of(width)
+    buffers, plan, first = [], [], 0
+    for _, lanes, order in parts:
+        left = [0, 1, 2]
+        stages = []
+        for d in order:
+            axis = left.index(d)
+            left.remove(d)
+            rest = tuple(cut[k] for k in left)
+            buffers.append(pltpu.VMEM((max(cut[d] - 1, 1), *rest, rows, lanes), jnp.float32))
+            buffers.append(pltpu.VMEM((*rest, rows, lanes), jnp.float32))
+            stages.append((d, axis, len(buffers) - 2, len(buffers) - 1, first))
+            first += cut[d] - 1
+        plan.append(stages)
+    half = rows // 2
+    out = pl.pallas_call(
+        functools.partial(combine_kernel, cut, parts, plan),
+        out_shape=jax.ShapeDtypeStruct((half * 2 * width // BLOCK, BLOCK), jnp.float32),
+        in_specs=[pl.BlockSpec(memory_space=pltpu.VMEM)],
+        out_specs=pl.BlockSpec(memory_space=pltpu.VMEM),
+        scratch_shapes=[
+            pltpu.VMEM((rows, width), jnp.float32),
+            pltpu.VMEM((half if half % 8 == 0 else rows, width), jnp.float32),
+            pltpu.SemaphoreType.DMA((first + 1,)),
+            pltpu.SemaphoreType.DMA((first + 1,)),
+            *buffers,
+        ],
+        compiler_params=pltpu.CompilerParams(
+            collective_id=0, has_side_effects=True, vmem_limit_bytes=32 << 20
+        ),
+    )(sums.reshape(*cut, rows, width))
+    return out.reshape(half, -1, BLOCK).transpose(1, 0, 2).reshape(-1, half * BLOCK)
 
 
 def per_device(grads, signs, kept):
-    sums = partial_sums(grads, signs, kept)
-    mine = lax.psum_scatter(sums, "param", scatter_dimension=0, tiled=True)
-    both = lax.all_to_all(mine, "trace", split_axis=0, concat_axis=1, tiled=True)
-    here = both.shape[0]
-    split = both.reshape(here, -1, BLOCK)
-    done = jnp.einsum("ftl,lc->tfc", split, lane_table(), precision=lax.Precision.HIGHEST)
-    return done.reshape(-1, here * BLOCK)
+    return combine(partial_sums(grads, signs, kept), lax.axis_size("param"))
 
 
 def solution(mesh):

time: 115 us -> 38.4 us (0.33)
  waiting for transfers between devices: 68.6 us -> 0 us
  Pallas kernels: 13.2 us -> 34.7 us
  blocking collectives: 16.5 us -> 0 us
  between operations: 13.4 us -> 0.01 us
    reduce_scatter x1 -> x0, waiting for transfers between devices: 68.6 us -> none  [per_device(): mine = lax.psum_scatter(sums, 'param', scatter_dimension=0, tiled=True)]
    pallas_call x0 -> x1, Pallas kernels: none -> 21.5 us  [combine(): pl.pallas_call(functools.partial(combine_kernel, cut, parts, plan), out_s...]
    all_to_all x1 -> x0, blocking collectives: 16.5 us -> none  [per_device(): lax.all_to_all(mine, 'trace', split_axis=0, concat_axis=1, tiled=True)]
    unnamed x1 -> x3, local copies, waits for them, and re-layouts: 0.65 us -> 1.86 us
  transfers between devices with their start and end apart: 1 -> 0, of which waited for: 1 -> 0; matrix products, arithmetic and copies ran while one was open for 0% -> 0% of each run, Pallas kernels for 0% -> 0%
where the time goes in v2:
time: 38.4 us; the launch traced here: 38.1 us
  Pallas kernels  34.7 us (90%)
  local copies, waits for them, and re-layouts  3.38 us (9%)
    pallas_call x1, Pallas kernels, combine(): pl.pallas_call(functools.partial(combine_kernel, cut, parts, plan), out_s...  21.5 us
    pallas_call x1, Pallas kernels, partial_sums(): pl.pallas_call(partial_kernel, out_shape=jax.ShapeDtypeStruct((keep, trac...  13.2 us
    unnamed x3, local copies, waits for them, and re-layouts  1.86 us
    broadcast_in_dim x1, local copies, waits for them, and re-layouts, partial_sums(): kept_wide = jnp.broadcast_to(kept[:, None], (keep, BLOCK))  1.52 us

profile of v2, /device:TPU:1, one launch (start us, length us, event | category | flops | bytes accessed | tf_op | source)
XLA Modules:
  0.0 38.1 jit_solution(10514968135507523373)
XLA Ops:
  0.0 1.5 %broadcast_in_dim.2.kept_ref = s32[512,128]{1,0:T(8,128)} broadcast(s32[512]{0:T(512)} %param.5), dimensions={0} | broadcast | bytes 264192 | tf_op jit(solution)/shard_map/broadcast_in_dim | solution.py:64
  1.5 13.2 %shard_map.37 = f32[512,512]{1,0:T(8,128)} custom-call(s32[512,128]{1,0:T(8,128)} %broadcast_in_dim.2.kept_ref, bf16[32768,128]{1,0:T(8,128)(2,1)} %bitcast.14, s32[8192,128]{1,0:T(8,128)} %bitcast.15), custom_call_target="tpu_custom_call" | custom-call | tf_op jit(solution)/shard_map/pallas_call | solution.py:65
  14.7 0.0 copy-start
  14.7 1.2 %copy-done = f32[512,512]{1,0:T(8,128)S(1)} copy-done((f32[512,512]{1,0:T(8,128)S(1)}, f32[512,512]{1,0:T(8,128)}, u32[]{:S(2)}) %copy-start) | copy-done | bytes 1048600
  15.9 21.5 %shard_map.38 = f32[128,128]{1,0:T(8,128)S(1)} custom-call(f32[4,2,2,32,512]{4,3,2,1,0:T(8,128)S(1)} %bitcast.12), custom_call_target="tpu_custom_call" | custom-call | tf_op jit(solution)/shard_map/pallas_call | solution.py:216
  37.4 0.6 %copy.6 = f32[8,2048]{1,0:T(8,128)} copy(f32[8,2048]{1,0:T(8,128)S(1)} %bitcast.13) | data formatting | bytes 131072
Async XLA Ops:
  14.7 1.2 %copy-start = (f32[512,512]{1,0:T(8,128)S(1)}, f32[512,512]{1,0:T(8,128)}, u32[]{:S(2)}) copy-start(f32[512,512]{1,0:T(8,128)} %shard_map.37) | copy-start | bytes 3145732

commit v3 on v2

--- a/solution.py
+++ b/solution.py
@@ -22,66 +22,6 @@
     return (1 - 2 * parity(value)).astype(jnp.float32).astype(jnp.bfloat16)
 
 
-def partial_kernel(kept_ref, x_ref, s_ref, o_ref, low_ref, wide_ref):
-    step = pl.program_id(0)
-    rows = s_ref.shape[0]
-    traces = x_ref.shape[0] // rows
-    kept = kept_ref[...]
-
-    @pl.when(step == 0)
-    def _():
-        lane = lax.broadcasted_iota(jnp.int32, kept.shape, 1)
-        for k in range(SUB):
-            low_ref[:, k * BLOCK:(k + 1) * BLOCK] = sign_of(kept & (lane + k * BLOCK))
-
-    upper = lax.axis_index("param") * pl.num_programs(0) + step
-    high = sign_of(kept & (upper * (SUB * BLOCK)))
-    table = low_ref[...] * jnp.concatenate([high] * SUB, axis=1)
-    wide_ref[...] = x_ref[...].astype(jnp.float32)
-    sign = (2 * s_ref[...] - 1).astype(jnp.float32)
-    signed = jnp.concatenate(
-        [(wide_ref[pl.ds(t, rows, stride=traces), :] * sign).astype(jnp.bfloat16) for t in range(traces)],
-        axis=1,
-    )
-    term = jnp.dot(table, signed, preferred_element_type=jnp.float32)
-
-    @pl.when(step == 0)
-    def _():
-        o_ref[...] = term
-
-    @pl.when(step > 0)
-    def _():
-        o_ref[...] += term
-
-
-def partial_sums(grads, signs, kept):
-    traces, local_size = grads.shape
-    keep = kept.shape[0]
-    blocks = local_size // BLOCK
-    rows = SUB * BLOCK
-    x = grads.reshape(traces, blocks, BLOCK).transpose(1, 0, 2).reshape(blocks * traces, BLOCK)
-    s = signs.reshape(blocks, BLOCK)
-    kept_wide = jnp.broadcast_to(kept[:, None], (keep, BLOCK))
-    return pl.pallas_call(
-        partial_kernel,
-        out_shape=jax.ShapeDtypeStruct((keep, traces * BLOCK), jnp.float32),
-        grid=(blocks // rows,),
-        in_specs=[
-            pl.BlockSpec((keep, BLOCK), lambda i: (0, 0)),
-            pl.BlockSpec((rows * traces, BLOCK), lambda i: (i, 0)),
-            pl.BlockSpec((rows, BLOCK), lambda i: (i, 0)),
-        ],
-        out_specs=pl.BlockSpec((keep, traces * BLOCK), lambda i: (0, 0)),
-        scratch_shapes=[
-            pltpu.VMEM((keep, rows), jnp.bfloat16),
-            pltpu.VMEM((rows * traces, BLOCK), jnp.float32),
-        ],
-        compiler_params=pltpu.CompilerParams(
-            dimension_semantics=("arbitrary",), vmem_limit_bytes=60 << 20
-        ),
-    )(kept_wide, x, s)
-
-
 def cut_of(groups):
     bits = groups.bit_length() - 1
     minor = bits // 3
@@ -101,7 +41,48 @@
     return ref.at[(slice(None),) * axis + (index,)]
 
 
-def combine_kernel(cut, parts, plan, sums_ref, o_ref, final_ref, other_ref, send_sem, recv_sem, *buffers):
+def partial_sums(kept_ref, x_hbm, s_hbm, x_ref, s_ref, x_sem, s_sem, wide_ref, low_ref, sums_ref):
+    steps, rows = s_ref.shape[0], s_ref.shape[1]
+    traces = x_ref.shape[1] // rows
+    groups = kept_ref.shape[0]
+    lane = lax.broadcasted_iota(jnp.int32, (BLOCK, BLOCK), 1)
+    kept = jnp.concatenate(
+        [jnp.broadcast_to(kept_ref[n:n + 1, :], (BLOCK, BLOCK)).T for n in range(groups)], axis=0
+    )
+    lane = jnp.concatenate([lane] * groups, axis=0)
+    for k in range(SUB):
+        low_ref[:, k * BLOCK:(k + 1) * BLOCK] = sign_of(kept & (lane + k * BLOCK))
+    base = lax.axis_index("param") * steps
+
+    def term(step):
+        pltpu.make_async_copy(x_hbm.at[step], x_ref.at[step], x_sem.at[step]).wait()
+        pltpu.make_async_copy(s_hbm.at[step], s_ref.at[step], s_sem.at[step]).wait()
+        high = sign_of(kept & ((base + step) * (SUB * BLOCK)))
+        table = low_ref[...] * jnp.concatenate([high] * SUB, axis=1)
+        wide_ref[...] = x_ref[step].astype(jnp.float32)
+        sign = (2 * s_ref[step] - 1).astype(jnp.float32)
+        signed = jnp.concatenate(
+            [(wide_ref[pl.ds(t, rows, stride=traces), :] * sign).astype(jnp.bfloat16) for t in range(traces)],
+            axis=1,
+        )
+        return jnp.dot(table, signed, preferred_element_type=jnp.float32).reshape(sums_ref.shape)
+
+    sums_ref[...] = term(0)
+
+    @pl.loop(1, steps)
+    def _(step):
+        sums_ref[...] += term(step)
+
+
+def fused_kernel(
+    cut, parts, plan, kept_ref, x_hbm, s_hbm, o_ref, x_ref, s_ref, x_sem, s_sem, wide_ref, low_ref, sums_ref,
+    final_ref, other_ref, send_sem, recv_sem, *buffers
+):
+    @pl.loop(0, s_ref.shape[0])
+    def _(step):
+        pltpu.make_async_copy(x_hbm.at[step], x_ref.at[step], x_sem.at[step]).start()
+        pltpu.make_async_copy(s_hbm.at[step], s_ref.at[step], s_sem.at[step]).start()
+
     own = lax.axis_index("param")
     core = lax.axis_index("trace")
     spans = (cut[1] * cut[2], cut[2], 1)
@@ -120,6 +101,7 @@
             )
             count += 1
     pl.semaphore_signal(barrier, inc=1, device_id={"trace": 1 - core}, device_id_type=pl.DeviceIdType.MESH)
+    partial_sums(kept_ref, x_hbm, s_hbm, x_ref, s_ref, x_sem, s_sem, wide_ref, low_ref, sums_ref)
     pl.semaphore_wait(barrier, count + 1)
 
     lanes = [pl.ds(low, width) for low, width, _ in parts]
@@ -194,8 +176,15 @@
     swap.wait_send()
 
 
-def combine(sums, groups):
-    keep, width = sums.shape
+def per_device(grads, signs, kept):
+    traces, local_size = grads.shape
+    groups = lax.axis_size("param")
+    keep, width = kept.shape[0], traces * BLOCK
+    blocks = local_size // BLOCK
+    chunk = SUB * BLOCK
+    steps = blocks // chunk
+    x = grads.reshape(traces, blocks, BLOCK).transpose(1, 0, 2).reshape(steps, chunk * traces, BLOCK)
+    s = signs.reshape(steps, chunk, BLOCK)
     cut = cut_of(groups)
     rows = keep // groups
     parts = parts_of(width)
@@ -214,11 +203,22 @@
         plan.append(stages)
     half = rows // 2
     out = pl.pallas_call(
-        functools.partial(combine_kernel, cut, parts, plan),
+        functools.partial(fused_kernel, cut, parts, plan),
         out_shape=jax.ShapeDtypeStruct((half * 2 * width // BLOCK, BLOCK), jnp.float32),
-        in_specs=[pl.BlockSpec(memory_space=pltpu.VMEM)],
+        in_specs=[
+            pl.BlockSpec(memory_space=pltpu.VMEM),
+            pl.BlockSpec(memory_space=pl.ANY),
+            pl.BlockSpec(memory_space=pl.ANY),
+        ],
         out_specs=pl.BlockSpec(memory_space=pltpu.VMEM),
         scratch_shapes=[
+            pltpu.VMEM(x.shape, x.dtype),
+            pltpu.VMEM(s.shape, s.dtype),
+            pltpu.SemaphoreType.DMA((steps,)),
+            pltpu.SemaphoreType.DMA((steps,)),
+            pltpu.VMEM(x.shape[1:], jnp.float32),
+            pltpu.VMEM((keep, chunk), jnp.bfloat16),
+            pltpu.VMEM((*cut, rows, width), jnp.float32),
             pltpu.VMEM((rows, width), jnp.float32),
             pltpu.VMEM((half if half % 8 == 0 else rows, width), jnp.float32),
             pltpu.SemaphoreType.DMA((first + 1,)),
@@ -226,14 +226,10 @@
             *buffers,
         ],
         compiler_params=pltpu.CompilerParams(
-            collective_id=0, has_side_effects=True, vmem_limit_bytes=32 << 20
+            collective_id=0, has_side_effects=True, vmem_limit_bytes=60 << 20
         ),
-    )(sums.reshape(*cut, rows, width))
+    )(kept.reshape(-1, BLOCK), x, s)
     return out.reshape(half, -1, BLOCK).transpose(1, 0, 2).reshape(-1, half * BLOCK)
-
-
-def per_device(grads, signs, kept):
-    return combine(partial_sums(grads, signs, kept), lax.axis_size("param"))
 
 
 def solution(mesh):

time: 38.4 us -> 33.1 us (0.86)
  Pallas kernels: 34.7 us -> 31.4 us
  local copies, waits for them, and re-layouts: 3.38 us -> 1.47 us
    pallas_call x2 -> x1, Pallas kernels: 34.7 us -> 31.4 us  [per_device(): pl.pallas_call(functools.partial(fused_kernel, cut, parts, plan), out_sha...]
    broadcast_in_dim x1 -> x0, local copies, waits for them, and re-layouts: 1.52 us -> none  [partial_sums(): kept_wide = jnp.broadcast_to(kept[:, None], (keep, BLOCK))]
    unnamed x3 -> x1, local copies, waits for them, and re-layouts: 1.86 us -> 1.47 us
where the time goes in v3:
time: 33.1 us; the launch traced here: 32.9 us
  Pallas kernels  31.4 us (95%)
  local copies, waits for them, and re-layouts  1.47 us (4%)
    pallas_call x1, Pallas kernels, per_device(): pl.pallas_call(functools.partial(fused_kernel, cut, parts, plan), out_sha...  31.4 us
    unnamed x1, local copies, waits for them, and re-layouts  1.47 us

profile of v3, /device:TPU:1, one launch (start us, length us, event | category | flops | bytes accessed | tf_op | source)
XLA Modules:
  0.0 32.9 jit_solution(17817001702697083972)
XLA Ops:
  0.0 31.4 %shard_map.37 = f32[128,128]{1,0:T(8,128)} custom-call(s32[4,128]{1,0:T(4,128)} %bitcast.15, bf16[8,4096,128]{2,1,0:T(8,128)(2,1)} %bitcast.12, s32[8,1024,128]{2,1,0:T(8,128)} %bitcast.13), custom_call_target="tpu_custom_call" | custom-call | tf_op jit(solution)/shard_map/pallas_call | solution.py:205
  31.4 1.5 %copy.6 = f32[8,2048]{1,0:T(8,128)} copy(f32[8,2048]{1,0:T(8,128)} %bitcast.14) | data formatting | bytes 131072

commit v4 on v3

--- a/solution.py
+++ b/solution.py
@@ -41,7 +41,7 @@
     return ref.at[(slice(None),) * axis + (index,)]
 
 
-def partial_sums(kept_ref, x_hbm, s_hbm, x_ref, s_ref, x_sem, s_sem, wide_ref, low_ref, sums_ref):
+def partial_sums(kept_ref, x_hbm, s_hbm, x_ref, s_ref, x_sem, s_sem, wide_refs, ready_refs, low_ref, sums_ref):
     steps, rows = s_ref.shape[0], s_ref.shape[1]
     traces = x_ref.shape[1] // rows
     groups = kept_ref.shape[0]
@@ -54,29 +54,40 @@
         low_ref[:, k * BLOCK:(k + 1) * BLOCK] = sign_of(kept & (lane + k * BLOCK))
     base = lax.axis_index("param") * steps
 
-    def term(step):
+    def prepare(step, slot):
         pltpu.make_async_copy(x_hbm.at[step], x_ref.at[step], x_sem.at[step]).wait()
         pltpu.make_async_copy(s_hbm.at[step], s_ref.at[step], s_sem.at[step]).wait()
+        wide_refs[slot][...] = x_ref[step].astype(jnp.float32)
+        sign = (2 * s_ref[step] - 1).astype(jnp.float32)
+        for t in range(traces):
+            ready_refs[slot][:, t * BLOCK:(t + 1) * BLOCK] = (
+                wide_refs[slot][pl.ds(t, rows, stride=traces), :] * sign
+            ).astype(jnp.bfloat16)
+
+    def term(step, slot):
         high = sign_of(kept & ((base + step) * (SUB * BLOCK)))
         table = low_ref[...] * jnp.concatenate([high] * SUB, axis=1)
-        wide_ref[...] = x_ref[step].astype(jnp.float32)
-        sign = (2 * s_ref[step] - 1).astype(jnp.float32)
-        signed = jnp.concatenate(
-            [(wide_ref[pl.ds(t, rows, stride=traces), :] * sign).astype(jnp.bfloat16) for t in range(traces)],
-            axis=1,
-        )
-        return jnp.dot(table, signed, preferred_element_type=jnp.float32).reshape(sums_ref.shape)
-
-    sums_ref[...] = term(0)
-
-    @pl.loop(1, steps)
-    def _(step):
-        sums_ref[...] += term(step)
+        found = jnp.dot(table, ready_refs[slot][...], preferred_element_type=jnp.float32)
+        return found.reshape(sums_ref.shape)
+
+    sums_ref[...] = jnp.zeros_like(sums_ref)
+    prepare(0, 0)
+
+    @pl.loop(0, steps // 2 - 1)
+    def _(pair):
+        prepare(2 * pair + 1, 1)
+        sums_ref[...] += term(2 * pair, 0)
+        prepare(2 * pair + 2, 0)
+        sums_ref[...] += term(2 * pair + 1, 1)
+
+    prepare(steps - 1, 1)
+    sums_ref[...] += term(steps - 2, 0)
+    sums_ref[...] += term(steps - 1, 1)
 
 
 def fused_kernel(
-    cut, parts, plan, kept_ref, x_hbm, s_hbm, o_ref, x_ref, s_ref, x_sem, s_sem, wide_ref, low_ref, sums_ref,
-    final_ref, other_ref, send_sem, recv_sem, *buffers
+    cut, parts, plan, kept_ref, x_hbm, s_hbm, o_ref, x_ref, s_ref, x_sem, s_sem, wide_a, wide_b,
+    ready_a, ready_b, low_ref, sums_ref, final_ref, other_ref, send_sem, recv_sem, *buffers
 ):
     @pl.loop(0, s_ref.shape[0])
     def _(step):
@@ -101,7 +112,9 @@
             )
             count += 1
     pl.semaphore_signal(barrier, inc=1, device_id={"trace": 1 - core}, device_id_type=pl.DeviceIdType.MESH)
-    partial_sums(kept_ref, x_hbm, s_hbm, x_ref, s_ref, x_sem, s_sem, wide_ref, low_ref, sums_ref)
+    partial_sums(
+        kept_ref, x_hbm, s_hbm, x_ref, s_ref, x_sem, s_sem, (wide_a, wide_b), (ready_a, ready_b), low_ref, sums_ref
+    )
     pl.semaphore_wait(barrier, count + 1)
 
     lanes = [pl.ds(low, width) for low, width, _ in parts]
@@ -217,6 +230,9 @@
             pltpu.SemaphoreType.DMA((steps,)),
             pltpu.SemaphoreType.DMA((steps,)),
             pltpu.VMEM(x.shape[1:], jnp.float32),
+            pltpu.VMEM(x.shape[1:], jnp.float32),
+            pltpu.VMEM((chunk, width), jnp.bfloat16),
+            pltpu.VMEM((chunk, width), jnp.bfloat16),
             pltpu.VMEM((keep, chunk), jnp.bfloat16),
             pltpu.VMEM((*cut, rows, width), jnp.float32),
             pltpu.VMEM((rows, width), jnp.float32),

time: 33.1 us -> 35.7 us (1.079)
  Pallas kernels: 31.4 us -> 34 us
    pallas_call x1, Pallas kernels: 31.4 us -> 34 us  [per_device(): pl.pallas_call(functools.partial(fused_kernel, cut, parts, plan), out_sha...]
where the time goes in v4:
time: 35.7 us; the launch traced here: 35.5 us
  Pallas kernels  34 us (95%)
  local copies, waits for them, and re-layouts  1.47 us (4%)
    pallas_call x1, Pallas kernels, per_device(): pl.pallas_call(functools.partial(fused_kernel, cut, parts, plan), out_sha...  34 us
    unnamed x1, local copies, waits for them, and re-layouts  1.47 us

profile of v4, /device:TPU:1, one launch (start us, length us, event | category | flops | bytes accessed | tf_op | source)
XLA Modules:
  0.0 35.5 jit_solution(8705880807753114579)
XLA Ops:
  0.0 34.0 %shard_map.37 = f32[128,128]{1,0:T(8,128)} custom-call(s32[4,128]{1,0:T(4,128)} %bitcast.15, bf16[8,4096,128]{2,1,0:T(8,128)(2,1)} %bitcast.12, s32[8,1024,128]{2,1,0:T(8,128)} %bitcast.13), custom_call_target="tpu_custom_call" | custom-call | tf_op jit(solution)/shard_map/pallas_call | solution.py:218
  34.0 1.5 %copy.6 = f32[8,2048]{1,0:T(8,128)} copy(f32[8,2048]{1,0:T(8,128)} %bitcast.14) | data formatting | bytes 131072

commit v5 on v3

--- a/solution.py
+++ b/solution.py
@@ -41,7 +41,7 @@
     return ref.at[(slice(None),) * axis + (index,)]
 
 
-def partial_sums(kept_ref, x_hbm, s_hbm, x_ref, s_ref, x_sem, s_sem, wide_ref, low_ref, sums_ref):
+def partial_sums(kept_ref, x_hbm, s_hbm, x_ref, s_ref, x_sem, s_sem, wide_ref, rest_ref, low_ref, early_ref, late_ref, send_early):
     steps, rows = s_ref.shape[0], s_ref.shape[1]
     traces = x_ref.shape[1] // rows
     groups = kept_ref.shape[0]
@@ -54,29 +54,42 @@
         low_ref[:, k * BLOCK:(k + 1) * BLOCK] = sign_of(kept & (lane + k * BLOCK))
     base = lax.axis_index("param") * steps
 
-    def term(step):
+    half = traces // 2
+
+    def table_of(step):
+        high = sign_of(kept & ((base + step) * (SUB * BLOCK)))
+        return low_ref[...] * jnp.concatenate([high] * SUB, axis=1)
+
+    early_ref[...] = jnp.zeros_like(early_ref)
+    late_ref[...] = jnp.zeros_like(late_ref)
+
+    @pl.loop(0, steps)
+    def _(step):
         pltpu.make_async_copy(x_hbm.at[step], x_ref.at[step], x_sem.at[step]).wait()
         pltpu.make_async_copy(s_hbm.at[step], s_ref.at[step], s_sem.at[step]).wait()
-        high = sign_of(kept & ((base + step) * (SUB * BLOCK)))
-        table = low_ref[...] * jnp.concatenate([high] * SUB, axis=1)
         wide_ref[...] = x_ref[step].astype(jnp.float32)
         sign = (2 * s_ref[step] - 1).astype(jnp.float32)
-        signed = jnp.concatenate(
-            [(wide_ref[pl.ds(t, rows, stride=traces), :] * sign).astype(jnp.bfloat16) for t in range(traces)],
-            axis=1,
-        )
-        return jnp.dot(table, signed, preferred_element_type=jnp.float32).reshape(sums_ref.shape)
-
-    sums_ref[...] = term(0)
-
-    @pl.loop(1, steps)
+        signed = [
+            (wide_ref[pl.ds(t, rows, stride=traces), :] * sign).astype(jnp.bfloat16) for t in range(traces)
+        ]
+        for t in range(half, traces):
+            rest_ref[step, :, (t - half) * BLOCK:(t - half + 1) * BLOCK] = signed[t]
+        early_ref[...] += jnp.dot(
+            table_of(step), jnp.concatenate(signed[:half], axis=1), preferred_element_type=jnp.float32
+        ).reshape(early_ref.shape)
+
+    send_early()
+
+    @pl.loop(0, steps)
     def _(step):
-        sums_ref[...] += term(step)
+        late_ref[...] += jnp.dot(
+            table_of(step), rest_ref[step], preferred_element_type=jnp.float32
+        ).reshape(late_ref.shape)
 
 
 def fused_kernel(
-    cut, parts, plan, kept_ref, x_hbm, s_hbm, o_ref, x_ref, s_ref, x_sem, s_sem, wide_ref, low_ref, sums_ref,
-    final_ref, other_ref, send_sem, recv_sem, *buffers
+    cut, parts, plan, kept_ref, x_hbm, s_hbm, o_ref, x_ref, s_ref, x_sem, s_sem, wide_ref, rest_ref, low_ref,
+    early_ref, late_ref, final_ref, other_ref, send_sem, recv_sem, *buffers
 ):
     @pl.loop(0, s_ref.shape[0])
     def _(step):
@@ -101,11 +114,9 @@
             )
             count += 1
     pl.semaphore_signal(barrier, inc=1, device_id={"trace": 1 - core}, device_id_type=pl.DeviceIdType.MESH)
-    partial_sums(kept_ref, x_hbm, s_hbm, x_ref, s_ref, x_sem, s_sem, wide_ref, low_ref, sums_ref)
-    pl.semaphore_wait(barrier, count + 1)
-
     lanes = [pl.ds(low, width) for low, width, _ in parts]
-    held = [sums_ref.at[:, :, :, :, lanes[n]] for n in range(len(parts))]
+    unit = parts[1][1]
+    held = [early_ref, late_ref.at[:, :, :, :, pl.ds(0, unit)], late_ref.at[:, :, :, :, pl.ds(unit, unit)]]
     flying = {}
     sent = []
 
@@ -127,8 +138,15 @@
         flying[n, stage] = copies
         sent.extend(copies)
 
-    for n in range(len(parts)):
-        launch(n, 0)
+    def send_early():
+        pl.semaphore_wait(barrier, count + 1)
+        launch(0, 0)
+
+    partial_sums(
+        kept_ref, x_hbm, s_hbm, x_ref, s_ref, x_sem, s_sem, wide_ref, rest_ref, low_ref, early_ref, late_ref, send_early
+    )
+    launch(1, 0)
+    launch(2, 0)
     for stage in range(3):
         for n in range(len(parts)):
             d, axis, slots, result, first = plan[n][stage]
@@ -217,8 +235,10 @@
             pltpu.SemaphoreType.DMA((steps,)),
             pltpu.SemaphoreType.DMA((steps,)),
             pltpu.VMEM(x.shape[1:], jnp.float32),
+            pltpu.VMEM((steps, chunk, width // 2), jnp.bfloat16),
             pltpu.VMEM((keep, chunk), jnp.bfloat16),
-            pltpu.VMEM((*cut, rows, width), jnp.float32),
+            pltpu.VMEM((*cut, rows, width // 2), jnp.float32),
+            pltpu.VMEM((*cut, rows, width // 2), jnp.float32),
             pltpu.VMEM((rows, width), jnp.float32),
             pltpu.VMEM((half if half % 8 == 0 else rows, width), jnp.float32),
             pltpu.SemaphoreType.DMA((first + 1,)),

time: 33.1 us -> 33.7 us (1.018)
  Pallas kernels: 31.4 us -> 31.8 us
    pallas_call x1, Pallas kernels: 31.4 us -> 31.8 us  [per_device(): pl.pallas_call(functools.partial(fused_kernel, cut, parts, plan), out_sha...]
where the time goes in v5:
time: 33.7 us; the launch traced here: 33.3 us
  Pallas kernels  31.8 us (94%)
  local copies, waits for them, and re-layouts  1.47 us (4%)
    pallas_call x1, Pallas kernels, per_device(): pl.pallas_call(functools.partial(fused_kernel, cut, parts, plan), out_sha...  31.8 us
    unnamed x1, local copies, waits for them, and re-layouts  1.47 us

profile of v5, /device:TPU:1, one launch (start us, length us, event | category | flops | bytes accessed | tf_op | source)
XLA Modules:
  0.0 33.3 jit_solution(4818968378291297218)
XLA Ops:
  0.0 31.8 %shard_map.37 = f32[128,128]{1,0:T(8,128)} custom-call(s32[4,128]{1,0:T(4,128)} %bitcast.15, bf16[8,4096,128]{2,1,0:T(8,128)(2,1)} %bitcast.12, s32[8,1024,128]{2,1,0:T(8,128)} %bitcast.13), custom_call_target="tpu_custom_call" | custom-call | tf_op jit(solution)/shard_map/pallas_call | solution.py:223
  31.8 1.5 %copy.6 = f32[8,2048]{1,0:T(8,128)} copy(f32[8,2048]{1,0:T(8,128)} %bitcast.14) | data formatting | bytes 131072
